TPU v7x, 256 devices: a whole 4x4x8 slice. The times are simulated.
256 devices in a mesh: seq: 32 (over z, y_hi, core), tp: 8 (over x, y_lo).
Axes of the slice: x: 4, y: 4 (y_hi: 2, y_lo: 2; y = y_hi * 2 + y_lo), z: 8, core: 2. Of those that a mesh axis runs over, the one named last changes fastest.
Arguments:
- stream: bfloat16 [8192, 2048], P('seq', 'tp'), may hold values from -16 to 16
- frames: int32 [8192], P('seq'), may hold values from 0 to 63, never falling along the last dimension, each value on 1 to 256 neighbouring positions
- fidelity: int32 [8192, 1], P('seq'), may hold values from 0 to 15; in each aligned block of 256 rows (0 to 255, 256 to 511, ...) at most 32 rows name the same one
- w_query: bfloat16 [2048, 2048], P(None, 'tp'), may hold values from -2 to 2
- w_key: bfloat16 [2048, 2048], P(None, 'tp'), may hold values from -2 to 2
- w_value: bfloat16 [2048, 2048], P(None, 'tp'), may hold values from -0.125 to 0.125
- w_output: bfloat16 [2048, 2048], P('tp'), may hold values from -0.125 to 0.125
- norm_gain: float32 [2048], replicated, may hold values from 0.1 to 1.9
- expert_gate: bfloat16 [32, 2048, 2816], P('seq', None, 'tp'), may hold values from -0.125 to 0.125
- expert_up: bfloat16 [32, 2048, 2816], P('seq', None, 'tp'), may hold values from -0.125 to 0.125
- expert_down: bfloat16 [32, 2816, 2048], P('seq', 'tp'), may hold values from -0.078125 to 0.078125
Outputs:
- result: bfloat16 [8192, 2048], P('seq', 'tp')
Inputs may be any that keep to these rules, and one draw needn't show every extreme that they name: `frames`: frame numbers never fall along the tokens; a frame holds 1 to 256 tokens, one exactly 256. `fidelity`: among the tokens of one index of seq (aligned blocks of 256 rows) no expert is named more than 32 times, a bound that some block reaches; every expert is named by some token.
All inputs are finite; a program needn't handle non-finite values.
Results may differ from a plain program's by a relative error of at most 0.02.
Values may be sent and summed in bfloat16 or wider, within the bound.
No kernel may reach another device: no remote copies, remote signals or barrier semaphores. Data moves between devices by JAX's collectives and lax.ppermute only.
A program may use at most 128 MiB of HBM per device.

v0:
```python
import math
import jax
import jax.numpy as jnp
from jax import lax
from jax.sharding import PartitionSpec as P

HEAD = 128
EXPERTS = 16
CAP = 32
big_negative = -1e30
norm_eps = 1e-05


def slot_rows(route_ids, tok_rows):
    onehot = (route_ids[:, None] == jnp.arange(EXPERTS, dtype=jnp.int32)[None, :]).astype(jnp.int32)
    places = jnp.sum(onehot * (jnp.cumsum(onehot, axis=0) - 1), axis=1)
    flat_slot = route_ids * CAP + places
    owner_table = (
        jnp.full((EXPERTS * CAP,), tok_rows, jnp.int32)
        .at[flat_slot]
        .set(jnp.arange(tok_rows, dtype=jnp.int32))
    )
    return (flat_slot, owner_table)


def shards(
    stream,
    frames,
    fidelity,
    w_query,
    w_key,
    w_value,
    w_output,
    norm_gain,
    expert_gate,
    expert_up,
    expert_down,
):
    tok_rows, slice_width = stream.shape
    tp_count = lax.axis_size("tp")
    seq_count = lax.axis_size("seq")
    width = slice_width * tp_count
    head_cols = w_query.shape[1]
    heads_here = head_cols // HEAD
    replicas = seq_count // EXPERTS
    col_start = lax.axis_index("tp") * slice_width
    gathered_rows = lax.all_gather(stream, "tp", axis=1, tiled=True)
    query_rows = jnp.dot(gathered_rows, w_query, preferred_element_type=jnp.float32).astype(
        jnp.bfloat16
    )
    key_rows = jnp.dot(gathered_rows, w_key, preferred_element_type=jnp.float32).astype(
        jnp.bfloat16
    )
    value_rows = jnp.dot(gathered_rows, w_value, preferred_element_type=jnp.float32).astype(
        jnp.bfloat16
    )
    query_heads = query_rows.reshape(tok_rows, heads_here, HEAD)
    score_scale = 1.0 / math.sqrt(HEAD)
    top_frame = jnp.max(frames)
    initial = (
        jnp.full((heads_here, tok_rows), big_negative, jnp.float32),
        jnp.zeros((heads_here, tok_rows), jnp.float32),
        jnp.zeros((tok_rows, heads_here, HEAD), jnp.float32),
    )
    key_piece = lax.all_gather(key_rows, "seq", axis=0, tiled=True)
    value_piece = lax.all_gather(value_rows, "seq", axis=0, tiled=True)
    frame_piece = lax.all_gather(frames, "seq", axis=0, tiled=True)

    def update(state):
        run_max, run_total, run_acc = state
        key_heads = key_piece.reshape(key_piece.shape[0], heads_here, HEAD)
        value_heads = value_piece.reshape(value_piece.shape[0], heads_here, HEAD)
        scores = (
            jnp.einsum("qhd,khd->hqk", query_heads, key_heads, preferred_element_type=jnp.float32)
            * score_scale
        )
        allowed = frame_piece[None, None, :] <= frames[None, :, None]
        scores = jnp.where(allowed, scores, big_negative)
        new_max = jnp.maximum(run_max, jnp.max(scores, axis=2))
        weights = jnp.where(allowed, jnp.exp(scores - new_max[:, :, None]), 0.0)
        new_total = jnp.sum(weights, axis=2)
        product = jnp.einsum(
            "hqk,khd->qhd",
            weights.astype(jnp.bfloat16),
            value_heads,
            preferred_element_type=jnp.float32,
        )
        return (new_max, new_total, product)

    run_max, run_total, run_acc = lax.cond(
        jnp.min(frame_piece) > top_frame, lambda unchanged: unchanged, update, initial
    )
    attended = (
        (run_acc / jnp.transpose(run_total)[:, :, None])
        .reshape(tok_rows, head_cols)
        .astype(jnp.bfloat16)
    )
    projected = jnp.dot(attended, w_output, preferred_element_type=jnp.float32)
    summed = lax.psum(projected.astype(jnp.bfloat16), "tp").astype(jnp.float32)
    mixed_full = (gathered_rows.astype(jnp.float32) + summed).astype(jnp.bfloat16)
    mixed_float = mixed_full.astype(jnp.float32)
    normed_full = (
        mixed_float
        * lax.rsqrt(jnp.mean(mixed_float * mixed_float, axis=1, keepdims=True) + norm_eps)
        * norm_gain[None, :]
    ).astype(jnp.bfloat16)
    mixed_rows = lax.dynamic_slice_in_dim(mixed_full, col_start, slice_width, 1)
    route_ids = fidelity[:, 0]
    flat_slot, owner_table = slot_rows(route_ids, tok_rows)
    padded = jnp.concatenate(
        [normed_full, jnp.zeros((1, normed_full.shape[1]), jnp.bfloat16)], axis=0
    )
    per_expert = jnp.take(padded, owner_table, axis=0).reshape(EXPERTS, CAP, normed_full.shape[1])
    sending = jnp.repeat(per_expert, replicas, axis=0)
    arrived = lax.all_to_all(sending, "seq", split_axis=0, concat_axis=0, tiled=True)
    flat_rows = arrived.reshape(-1, width)
    gate_act = jnp.dot(flat_rows, expert_gate[0], preferred_element_type=jnp.float32)
    up_act = jnp.dot(flat_rows, expert_up[0], preferred_element_type=jnp.float32)
    hidden = (jax.nn.silu(gate_act) * up_act).astype(jnp.bfloat16)
    lowered = jnp.dot(hidden, expert_down[0], preferred_element_type=jnp.float32).reshape(
        arrived.shape[0], arrived.shape[1], width
    )
    results = lax.psum(lowered.astype(jnp.bfloat16), "tp")
    returned = lax.all_to_all(results, "seq", split_axis=0, concat_axis=0, tiled=True)
    out_width = returned.shape[2]
    combined = jnp.sum(
        returned.astype(jnp.float32).reshape(EXPERTS, replicas, CAP, out_width), axis=1
    ).reshape(EXPERTS * CAP, out_width)
    own_rows = jnp.take(combined, flat_slot, axis=0)
    own_rows = lax.dynamic_slice_in_dim(own_rows, col_start, slice_width, 1)
    return (mixed_rows.astype(jnp.float32) + own_rows).astype(jnp.bfloat16)


def solution(mesh):
    return jax.shard_map(
        shards,
        mesh=mesh,
        in_specs=(
            P("seq", "tp"),
            P("seq"),
            P("seq", None),
            P(None, "tp"),
            P(None, "tp"),
            P(None, "tp"),
            P("tp", None),
            P(),
            P("seq", None, "tp"),
            P("seq", None, "tp"),
            P("seq", "tp", None),
        ),
        out_specs=P("seq", "tp"),
        check_vma=False,
    )
```

profile of v0, /device:TPU:4, one launch (start us, length us, event | category | flops | bytes accessed | tf_op | source)
XLA Modules:
  0.0 785.2 jit_solution(12655478996595157357)
XLA Ops:
  7.3 47.9 %all-gather.5.cloned.1.call-done = bf16[256,2048]{1,0:T(8,128)(2,1)} async-done(((bf16[256,256]{1,0:T(8,128)(2,1)}), bf16[256,2048]{1,0:T(8,128)(2,1)}) %all-gather.5.cloned.1.call-update) | async-done | bytes 1048592 | tf_op jit(solution)/shard_map/all_gather | solution.py:47
  55.2 2.7 convolution_convert_fusion.3
  58.0 2.6 convolution_convert_fusion.2
  61.4 44.6 %all-gather = s32[32,1,256]{2,1,0:T(1,128)} all-gather(s32[1,1,256]{2,1,0:T(1,128)S(1)} %bitcast.91), channel_id=1, replica_groups=mesh['seq'=32,'tp'=8] {'seq'}, dimensions={0}, use_global_device_ids=true | all-gather | bytes 33792 | tf_op jit(solution)/shard_map/all_gather | solution.py:67
  109.9 38.8 %all-gather.7.cloned.1.call-done = bf16[8192,256]{1,0:T(8,128)(2,1)} async-done(((bf16[256,256]{1,0:T(8,128)(2,1)}), bf16[8192,256]{1,0:T(8,128)(2,1)}) %all-gather.7.cloned.1.call-update) | async-done | bytes 4194320 | tf_op jit(solution)/shard_map/all_gather | solution.py:65
  148.6 86.3 %all-gather.9.cloned.1.call-done = bf16[8192,256]{1,0:T(8,128)(2,1)} async-done(((bf16[256,256]{1,0:T(8,128)(2,1)}), bf16[8192,256]{1,0:T(8,128)(2,1)}) %all-gather.9.cloned.1.call-update) | async-done | bytes 4194320 | tf_op jit(solution)/shard_map/all_gather | solution.py:66
  234.9 36.7 %conditional.1 = (f32[2,256]{1,0:T(2,128)S(1)}, f32[256,2,128]{0,2,1:T(8,128)}) conditional(s32[]{:T(128)} %convert_element_type.58, (s32[8192]{0:T(1024)}, s32[256]{0:T(256)S(1)}, bf16[256,256]{1,0:T(8,128)(2,1)}, bf16[8192,256]{1,0:T(8,128)(2,1)}, bf16[8192,256]{1,0:T(8,128)(2,1)}) %tuple.33, () %tuple.14), branch_computations={%region_2.5_spmd, %region_5.6_spmd} | conditional | flops 2204106240 | bytes 143570000 | solution.py:90
  234.9 2.1 broadcast_compare_fusion
  237.0 12.8 %fusion = (f32[2,256]{1,0:T(2,128)S(1)}, f32[2,256,8192]{2,1,0:T(8,128)}) fusion(pred[256,8192]{1,0:T(8,128)(4,1)S(1)} %broadcast_compare_fusion, bf16[8192,256]{1,0:T(8,128)(2,1)} %get-tuple-element.19, bf16[256,256]{1,0:T(8,128)(2,1)} %get-tuple-element.18), kind=kOutput, calls=%fused_computation.5 | convolution fusion | flops 1086324224 | bytes 23201792 | tf_op jit(solution)/shard_map/cond/branch_0_fun/qhd,khd->hqk/dot_general | solution.py:74
  249.8 9.2 %fusion.2 = f32[2,256]{1,0:T(2,128)S(1)} fusion(f32[2,256,8192]{2,1,0:T(8,128)} %get-tuple-element.31, f32[2,256]{1,0:T(2,128)S(1)} %broadcast_maximum_fusion, pred[256,8192]{1,0:T(8,128)(4,1)} %copy-done.3), kind=kLoop, calls=%fused_computation.7 | loop fusion | flops 20971008 | bytes 18878464 | tf_op jit(solution)/shard_map/cond/branch_0_fun/reduce_sum | solution.py:81
  259.0 2.1 copy-done.1
  261.1 8.8 %fusion.11 = f32[256,2,128]{2,0,1:T(8,128)} fusion(f32[2,256,8192]{2,1,0:T(8,128)S(1)} %copy-done.1, f32[2,256]{1,0:T(2,128)S(1)} %broadcast_maximum_fusion, pred[256,8192]{1,0:T(8,128)(4,1)} %copy-done.3, bf16[8192,256]{1,0:T(8,128)(2,1)} %get-tuple-element.20), kind=kOutput, calls=%fused_computation.16 | convolution fusion | flops 1094713344 | bytes 23332864 | tf_op jit(solution)/shard_map/cond/branch_0_fun/hqk,khd->qhd/dot_general | solution.py:82
  269.9 1.8 copy.28
  277.2 75.0 %all-reduce.4.cloned.1.call-done = bf16[256,2048]{1,0:T(8,128)(2,1)} async-done(((bf16[256,2048]{1,0:T(8,128)(2,1)}), bf16[256,2048]{1,0:T(8,128)(2,1)}) %all-reduce.4.cloned.1.call-update) | async-done | bytes 1048592 | tf_op jit(solution)/shard_map/psum | solution.py:99
  355.4 3.3 gather_fusion
  358.7 1.8 broadcast_select_fusion
  361.2 105.9 %all_to_all.10 = bf16[32,32,2048]{2,1,0:T(8,128)(2,1)S(1)} all-to-all(bf16[32,32,2048]{2,1,0:T(8,128)(2,1)S(1)} %bitcast.84), channel_id=1, replica_groups=mesh['seq'=32,'tp'=8] {'seq'}, dimensions={0} | all-to-all | bytes 8388608 | tf_op jit(solution)/shard_map/all_to_all | solution.py:115
  468.8 1.8 fusion.28
  471.0 4.3 convolution_convert_fusion
  475.3 185.1 %all-reduce.6.cloned.1.call-done = bf16[32,32,2048]{2,1,0:T(8,128)(2,1)} async-done(((bf16[32,32,2048]{2,1,0:T(8,128)(2,1)}), bf16[32,32,2048]{2,1,0:T(8,128)(2,1)}) %all-reduce.6.cloned.1.call-update) | async-done | bytes 4194320 | tf_op jit(solution)/shard_map/psum | solution.py:123
  660.4 9.9 %all-to-all-start.1 = ((bf16[32,32,2048]{2,1,0:T(8,128)(2,1)}), bf16[32,32,2048]{2,1,0:T(8,128)(2,1)}, u32[]{:S(2)}, u32[]{:S(2)}) async-start(bf16[32,32,2048]{2,1,0:T(8,128)(2,1)} %all-reduce.6.cloned.1.call-done), calls=%async_computation.1 | async-start | bytes 8388608 | tf_op jit(solution)/shard_map/all_to_all | solution.py:124
  670.3 96.5 %all-to-all-done.1 = bf16[32,32,2048]{2,1,0:T(8,128)(2,1)} async-done(((bf16[32,32,2048]{2,1,0:T(8,128)(2,1)}), bf16[32,32,2048]{2,1,0:T(8,128)(2,1)}, u32[]{:S(2)}, u32[]{:S(2)}) %all-to-all-start.1) | async-done | bytes 4194336 | tf_op jit(solution)/shard_map/all_to_all | solution.py:124
  766.8 5.6 convert_reduce_fusion
  772.4 4.6 gather_fusion.1
  (63 shorter events, 17.1 us)
Async XLA Ops:
  6.5 464.5 %copy-start = (bf16[1,352,2048]{2,1,0:T(8,128)(2,1)S(1)}, bf16[1,352,2048]{2,1,0:T(8,128)(2,1)}, u32[]{:S(2)}) copy-start(bf16[1,352,2048]{2,1,0:T(8,128)(2,1)} %param.23) | copy-start | bytes 4325380
  6.5 54.2 %copy-start.7 = (s32[256]{0:T(256)S(1)}, s32[256]{0:T(256)}, u32[]{:S(2)}) copy-start(s32[256]{0:T(256)} %param.14) | copy-start | bytes 3076
  6.5 102.2 %copy-start.5 = (bf16[2048,256]{1,0:T(8,128)(2,1)S(1)}, bf16[2048,256]{1,0:T(8,128)(2,1)}, u32[]{:S(2)}) copy-start(bf16[2048,256]{1,0:T(8,128)(2,1)} %param.16) | copy-start | bytes 3145732
  6.5 48.7 %all-gather.5.cloned.1.call-start = ((), (), s32[]{:S(2)}) async-start(), calls=%async_computation.2 | async-start | bytes 1179648 | tf_op jit(solution)/shard_map/all_gather | solution.py:47
  7.3 141.4 %all-gather.7.cloned.1.call-start = ((), (), s32[]{:S(2)}) async-start(), calls=%async_computation.3 | async-start | bytes 4325376 | tf_op jit(solution)/shard_map/all_gather | solution.py:65
  55.2 53.5 %copy-start.2 = (bf16[256,2048]{1,0:T(8,128)(2,1)S(1)}, bf16[256,2048]{1,0:T(8,128)(2,1)}, u32[]{:S(2)}) copy-start(bf16[256,2048]{1,0:T(8,128)(2,1)} %all-gather.5.cloned.1.call-done) | copy-start | bytes 3145732
  58.0 177.0 %all-gather.9.cloned.1.call-start = ((), (), s32[]{:S(2)}) async-start(), calls=%async_computation.4 | async-start | bytes 4325376 | tf_op jit(solution)/shard_map/all_gather | solution.py:66
  60.7 291.5 %all-reduce.4.cloned.1.call-start = ((), (), s32[]{:S(2)}) async-start(), calls=%async_computation.5 | async-start | bytes 2097152 | tf_op jit(solution)/shard_map/psum | solution.py:99
  234.9 37.7 %copy-start.6 = (bf16[256,2048]{1,0:T(8,128)(2,1)S(1)}, bf16[256,2048]{1,0:T(8,128)(2,1)}, u32[]{:S(2)}) copy-start(bf16[256,2048]{1,0:T(8,128)(2,1)} %param.19) | copy-start | bytes 3145732
  234.9 39.3 %copy-start.8 = (s32[256,1]{0,1:T(1,128)S(1)}, s32[256,1]{0,1:T(1,128)}, u32[]{:S(2)}) copy-start(s32[256,1]{0,1:T(1,128)} %param.15) | copy-start | bytes 3076
  237.0 12.8 %copy-start.3 = (pred[256,8192]{1,0:T(8,128)(4,1)}, pred[256,8192]{1,0:T(8,128)(4,1)S(1)}, u32[]{:S(2)}) copy-start(pred[256,8192]{1,0:T(8,128)(4,1)S(1)} %broadcast_compare_fusion) | copy-start | bytes 6291460 | tf_op jit(solution)/shard_map/cond
  249.8 11.3 %copy-start.1 = (f32[2,256,8192]{2,1,0:T(8,128)S(1)}, f32[2,256,8192]{2,1,0:T(8,128)}, u32[]{:S(2)}) copy-start(f32[2,256,8192]{2,1,0:T(8,128)} %get-tuple-element.31) | copy-start | bytes 50331652 | tf_op jit(solution)/shard_map/cond
  271.7 83.3 %copy-start.9 = (f32[2048]{0:T(1024)S(1)}, f32[2048]{0:T(1024)}, u32[]{:S(2)}) copy-start(f32[2048]{0:T(1024)} %param.20) | copy-start | bytes 24580
  274.2 386.2 %all-reduce.6.cloned.1.call-start = ((), (), s32[]{:S(2)}) async-start(), calls=%async_computation.6 | async-start | bytes 8388608 | tf_op jit(solution)/shard_map/psum | solution.py:123
  353.9 1.1 copy-start.4
  361.1 105.9 %copy-start.11 = (bf16[1,2048,352]{1,2,0:T(8,128)(2,1)S(1)}, bf16[1,2048,352]{1,2,0:T(8,128)(2,1)}, u32[]{:S(2)}) copy-start(bf16[1,2048,352]{1,2,0:T(8,128)(2,1)} %param.21) | copy-start | bytes 4325380
  467.1 1.8 copy-start.12
  660.4 106.4 %all-to-all-start.1 = ((bf16[32,32,2048]{2,1,0:T(8,128)(2,1)}), bf16[32,32,2048]{2,1,0:T(8,128)(2,1)}, u32[]{:S(2)}, u32[]{:S(2)}) async-start(bf16[32,32,2048]{2,1,0:T(8,128)(2,1)} %all-reduce.6.cloned.1.call-done), calls=%async_computation.1 | async-start | bytes 8388608 | tf_op jit(solution)/shard_map/all_to_all | solution.py:124
  772.4 4.6 copy-start.10
Sparse Core Ops, SparseCore 0:
  9.1 46.1 all-gather.4
  58.1 90.4 all-gather.6
  151.4 83.4 all-gather.8
  274.3 77.8 all-reduce.3
  475.4 184.8 all-reduce.5
where the time goes:
time: 786 us; the launch traced here: 785 us
  waiting for transfers between devices  530 us (67%)
  blocking collectives  151 us (19%)
  matrix products  37.3 us (5%)
  other arithmetic  26.8 us (3%)
  local copies, waits for them, and re-layouts  15.5 us (2%)
  between operations  14.6 us (2%)
  starting transfers between devices  10.1 us (1%)
    psum x1, waiting for transfers between devices, shards(): results = lax.psum(lowered.astype(jnp.bfloat16), 'tp')  185 us
    all_to_all x1, blocking collectives, shards(): lax.all_to_all(sending, 'seq', split_axis=0, concat_axis=0, tiled=True)  106 us
    all_to_all x1, waiting for transfers between devices, shards(): lax.all_to_all(results, 'seq', split_axis=0, concat_axis=0, tiled=True)  96.5 us
    all_gather x1, waiting for transfers between devices, shards(): value_piece = lax.all_gather(value_rows, 'seq', axis=0, tiled=True)  86.3 us
    psum x1, waiting for transfers between devices, shards(): summed = lax.psum(projected.astype(jnp.bfloat16), 'tp').astype(jnp.float32)  75 us
    all_gather x1, waiting for transfers between devices, shards(): gathered_rows = lax.all_gather(stream, 'tp', axis=1, tiled=True)  47.9 us
    all_gather x1, blocking collectives, shards(): frame_piece = lax.all_gather(frames, 'seq', axis=0, tiled=True)  44.6 us
    all_gather x1, waiting for transfers between devices, shards(): key_piece = lax.all_gather(key_rows, 'seq', axis=0, tiled=True)  38.8 us
  transfers between devices with their start and end apart: 6, of which 6 were waited for; matrix products, arithmetic and copies ran while one was open for 1% of the time, Pallas kernels for 0%

commit v1 on v0

--- a/solution.py
+++ b/solution.py
@@ -62,8 +62,11 @@
         jnp.zeros((heads_here, tok_rows), jnp.float32),
         jnp.zeros((tok_rows, heads_here, HEAD), jnp.float32),
     )
-    key_piece = lax.all_gather(key_rows, "seq", axis=0, tiled=True)
-    value_piece = lax.all_gather(value_rows, "seq", axis=0, tiled=True)
+    key_piece, value_piece = jnp.split(
+        lax.all_gather(jnp.concatenate([key_rows, value_rows], axis=1), "seq", axis=0, tiled=True),
+        [key_rows.shape[1]],
+        axis=1,
+    )
     frame_piece = lax.all_gather(frames, "seq", axis=0, tiled=True)
 
     def update(state):

time: 786 us -> 720 us (0.916)
  waiting for transfers between devices: 530 us -> 468 us
    all_gather x2 -> x1, waiting for transfers between devices: 125 us -> 63.2 us  [shards(): lax.all_gather(jnp.concatenate([key_rows, value_rows], axis=1), 'seq', ax...]
  transfers between devices with their start and end apart: 6 -> 5, of which waited for: 6 -> 5; matrix products, arithmetic and copies ran while one was open for 1% -> 1% of each run, Pallas kernels for 0% -> 0%
where the time goes in v1:
time: 720 us
  waiting for transfers between devices  468 us (65%)
  blocking collectives  151 us (21%)
  matrix products  31.3 us (4%)
  other arithmetic  27.1 us (4%)
  local copies, waits for them, and re-layouts  18.4 us (3%)
  between operations  14.6 us (2%)
  starting transfers between devices  9.81 us (1%)
    psum x1, waiting for transfers between devices, shards(): results = lax.psum(lowered.astype(jnp.bfloat16), 'tp')  185 us
    all_to_all x1, blocking collectives, shards(): lax.all_to_all(sending, 'seq', split_axis=0, concat_axis=0, tiled=True)  106 us
    all_to_all x1, waiting for transfers between devices, shards(): lax.all_to_all(results, 'seq', split_axis=0, concat_axis=0, tiled=True)  96.7 us
    psum x1, waiting for transfers between devices, shards(): summed = lax.psum(projected.astype(jnp.bfloat16), 'tp').astype(jnp.float32)  74.4 us
    all_gather x1, waiting for transfers between devices, shards(): lax.all_gather(jnp.concatenate([key_rows, value_rows], axis=1), 'seq', ax...  63.2 us
    all_gather x1, waiting for transfers between devices, shards(): gathered_rows = lax.all_gather(stream, 'tp', axis=1, tiled=True)  47.9 us
    all_gather x1, blocking collectives, shards(): frame_piece = lax.all_gather(frames, 'seq', axis=0, tiled=True)  44.6 us
  transfers between devices with their start and end apart: 5, of which 5 were waited for; matrix products, arithmetic and copies ran while one was open for 1% of the time, Pallas kernels for 0%

profile of v1, /device:TPU:4, one launch (start us, length us, event | category | flops | bytes accessed | tf_op | source)
XLA Modules:
  0.0 719.8 jit_solution(13088445047978022656)
XLA Ops:
  7.3 47.9 %all-gather.4.cloned.1.call-done = bf16[256,2048]{1,0:T(8,128)(2,1)} async-done(((bf16[256,256]{1,0:T(8,128)(2,1)}), bf16[256,2048]{1,0:T(8,128)(2,1)}) %all-gather.4.cloned.1.call-update) | async-done | bytes 1048592 | tf_op jit(solution)/shard_map/all_gather | solution.py:47
  55.2 2.1 convolution_convert_fusion.2
  57.4 2.1 convolution_convert_fusion.3
  60.9 44.6 %all-gather = s32[32,1,256]{2,1,0:T(1,128)} all-gather(s32[1,1,256]{2,1,0:T(1,128)S(1)} %bitcast.79), channel_id=1, replica_groups=mesh['seq'=32,'tp'=8] {'seq'}, dimensions={0}, use_global_device_ids=true | all-gather | bytes 33792 | tf_op jit(solution)/shard_map/all_gather | solution.py:70
  109.4 63.2 %all-gather.6.cloned.1.call-done = bf16[8192,512]{0,1:T(8,128)(2,1)} async-done(((bf16[256,512]{0,1:T(8,128)(2,1)}), bf16[8192,512]{0,1:T(8,128)(2,1)}) %all-gather.6.cloned.1.call-update) | async-done | bytes 8388624 | tf_op jit(solution)/shard_map/all_gather | solution.py:66
  172.6 34.1 %conditional.1 = (f32[2,256]{1,0:T(2,128)S(1)}, f32[256,2,128]{0,2,1:T(8,128)}) conditional(s32[]{:T(128)} %convert_element_type.58, (s32[8192]{0:T(1024)}, s32[256]{0:T(256)S(1)}, bf16[256,256]{1,0:T(8,128)(2,1)}, bf16[8192,512]{0,1:T(8,128)(2,1)}) %tuple.33, () %tuple.14), branch_computations={%region_2.5_spmd, %region_5.6_spmd} | conditional | flops 2204106240 | bytes 93762632 | solution.py:93
  172.6 2.1 broadcast_compare_fusion
  174.7 4.8 fusion.32
  179.5 7.9 %fusion = (f32[2,256]{1,0:T(2,128)S(1)}, f32[2,256,8192]{2,1,0:T(8,128)}) fusion(pred[256,8192]{1,0:T(8,128)(4,1)S(1)} %broadcast_compare_fusion, bf16[8192,2,128]{0,2,1:T(8,128)(2,1)S(1)} %bitcast.75, bf16[256,256]{1,0:T(8,128)(2,1)S(1)} %copy-done.6), kind=kOutput, calls=%fused_computation.5 | convolution fusion | flops 1086324224 | bytes 23201792 | tf_op jit(solution)/shard_map/cond/branch_0_fun/qhd,khd->hqk/dot_general | solution.py:77
  187.4 8.7 %fusion.6 = f32[256,2,128]{2,0,1:T(8,128)} fusion(bf16[8192,2,128]{0,2,1:T(8,128)(2,1)S(1)} %bitcast.74, f32[2,256,8192]{2,1,0:T(8,128)} %get-tuple-element.37, f32[2,256]{1,0:T(2,128)S(1)} %broadcast_maximum_fusion, pred[256,8192]{1,0:T(8,128)(4,1)S(1)} %broadcast_compare_fusion), kind=kOutput, calls=%fused_computation.11 | convolution fusion | flops 1094713344 | bytes 23332864 | tf_op jit(solution)/shard_map/cond/branch_0_fun/hqk,khd->qhd/dot_general | solution.py:85
  196.1 1.8 copy.29
  197.9 8.8 %fusion.2 = f32[2,256]{1,0:T(2,128)S(1)} fusion(f32[2,256,8192]{2,1,0:T(8,128)} %get-tuple-element.37, f32[2,256]{1,0:T(2,128)S(1)} %broadcast_maximum_fusion, pred[256,8192]{1,0:T(8,128)(4,1)} %copy-done.2), kind=kLoop, calls=%fused_computation.7 | loop fusion | flops 20971008 | bytes 18878464 | tf_op jit(solution)/shard_map/cond/branch_0_fun/reduce_sum | solution.py:84
  212.5 74.4 %all-reduce.4.cloned.1.call-done = bf16[256,2048]{1,0:T(8,128)(2,1)} async-done(((bf16[256,2048]{1,0:T(8,128)(2,1)}), bf16[256,2048]{1,0:T(8,128)(2,1)}) %all-reduce.4.cloned.1.call-update) | async-done | bytes 1048592 | tf_op jit(solution)/shard_map/psum | solution.py:102
  290.1 3.3 gather_fusion
  293.4 1.8 broadcast_select_fusion
  295.8 105.9 %all_to_all.10 = bf16[32,32,2048]{2,1,0:T(8,128)(2,1)S(1)} all-to-all(bf16[32,32,2048]{2,1,0:T(8,128)(2,1)S(1)} %bitcast.70), channel_id=1, replica_groups=mesh['seq'=32,'tp'=8] {'seq'}, dimensions={0} | all-to-all | bytes 8388608 | tf_op jit(solution)/shard_map/all_to_all | solution.py:118
  401.7 1.7 fusion.20
  403.5 1.8 fusion.22
  405.7 4.3 convolution_convert_fusion
  410.0 185.0 %all-reduce.6.cloned.1.call-done = bf16[32,32,2048]{2,1,0:T(8,128)(2,1)} async-done(((bf16[32,32,2048]{2,1,0:T(8,128)(2,1)}), bf16[32,32,2048]{2,1,0:T(8,128)(2,1)}) %all-reduce.6.cloned.1.call-update) | async-done | bytes 4194320 | tf_op jit(solution)/shard_map/psum | solution.py:126
  595.1 9.7 %all-to-all-start.1 = ((bf16[32,32,2048]{2,1,0:T(8,128)(2,1)}), bf16[32,32,2048]{2,1,0:T(8,128)(2,1)}, u32[]{:S(2)}, u32[]{:S(2)}) async-start(bf16[32,32,2048]{2,1,0:T(8,128)(2,1)} %all-reduce.6.cloned.1.call-done), calls=%async_computation.1 | async-start | bytes 8388608 | tf_op jit(solution)/shard_map/all_to_all | solution.py:127
  604.8 96.7 %all-to-all-done.1 = bf16[32,32,2048]{2,1,0:T(8,128)(2,1)} async-done(((bf16[32,32,2048]{2,1,0:T(8,128)(2,1)}), bf16[32,32,2048]{2,1,0:T(8,128)(2,1)}, u32[]{:S(2)}, u32[]{:S(2)}) %all-to-all-start.1) | async-done | bytes 4194336 | tf_op jit(solution)/shard_map/all_to_all | solution.py:127
  701.4 5.6 convert_reduce_fusion
  707.0 4.6 gather_fusion.1
  (62 shorter events, 16.2 us)
Async XLA Ops:
  6.5 399.2 %copy-start = (bf16[1,352,2048]{2,1,0:T(8,128)(2,1)S(1)}, bf16[1,352,2048]{2,1,0:T(8,128)(2,1)}, u32[]{:S(2)}) copy-start(bf16[1,352,2048]{2,1,0:T(8,128)(2,1)} %param.23) | copy-start | bytes 4325380
  6.5 53.7 %copy-start.7 = (s32[256]{0:T(256)S(1)}, s32[256]{0:T(256)}, u32[]{:S(2)}) copy-start(s32[256]{0:T(256)} %param.14) | copy-start | bytes 3076
  6.5 101.8 %copy-start.4 = (bf16[2048,256]{1,0:T(8,128)(2,1)S(1)}, bf16[2048,256]{1,0:T(8,128)(2,1)}, u32[]{:S(2)}) copy-start(bf16[2048,256]{1,0:T(8,128)(2,1)} %param.16) | copy-start | bytes 3145732
  6.5 48.7 %all-gather.4.cloned.1.call-start = ((), (), s32[]{:S(2)}) async-start(), calls=%async_computation.2 | async-start | bytes 1179648 | tf_op jit(solution)/shard_map/all_gather | solution.py:47
  7.3 165.4 %all-gather.6.cloned.1.call-start = ((), (), s32[]{:S(2)}) async-start(), calls=%async_computation.3 | async-start | bytes 8650752 | tf_op jit(solution)/shard_map/all_gather | solution.py:66
  55.2 53.1 %copy-start.1 = (bf16[256,2048]{1,0:T(8,128)(2,1)S(1)}, bf16[256,2048]{1,0:T(8,128)(2,1)}, u32[]{:S(2)}) copy-start(bf16[256,2048]{1,0:T(8,128)(2,1)} %all-gather.4.cloned.1.call-done) | copy-start | bytes 3145732
  60.2 226.6 %all-reduce.4.cloned.1.call-start = ((), (), s32[]{:S(2)}) async-start(), calls=%async_computation.4 | async-start | bytes 2097152 | tf_op jit(solution)/shard_map/psum | solution.py:102
  172.6 35.1 %copy-start.5 = (bf16[256,2048]{1,0:T(8,128)(2,1)S(1)}, bf16[256,2048]{1,0:T(8,128)(2,1)}, u32[]{:S(2)}) copy-start(bf16[256,2048]{1,0:T(8,128)(2,1)} %param.19) | copy-start | bytes 3145732
  172.6 36.7 %copy-start.8 = (s32[256,1]{0,1:T(1,128)S(1)}, s32[256,1]{0,1:T(1,128)}, u32[]{:S(2)}) copy-start(s32[256,1]{0,1:T(1,128)} %param.15) | copy-start | bytes 3076
  174.7 12.7 %copy-start.2 = (pred[256,8192]{1,0:T(8,128)(4,1)}, pred[256,8192]{1,0:T(8,128)(4,1)S(1)}, u32[]{:S(2)}) copy-start(pred[256,8192]{1,0:T(8,128)(4,1)S(1)} %broadcast_compare_fusion) | copy-start | bytes 6291460 | tf_op jit(solution)/shard_map/cond
  174.7 4.8 copy-start.6
  206.8 82.9 %copy-start.9 = (f32[2048]{0:T(1024)S(1)}, f32[2048]{0:T(1024)}, u32[]{:S(2)}) copy-start(f32[2048]{0:T(1024)} %param.20) | copy-start | bytes 24580
  209.3 385.8 %all-reduce.6.cloned.1.call-start = ((), (), s32[]{:S(2)}) async-start(), calls=%async_computation.5 | async-start | bytes 8388608 | tf_op jit(solution)/shard_map/psum | solution.py:126
  288.6 1.1 copy-start.3
  295.8 105.9 %copy-start.11 = (bf16[1,2048,352]{1,2,0:T(8,128)(2,1)S(1)}, bf16[1,2048,352]{1,2,0:T(8,128)(2,1)}, u32[]{:S(2)}) copy-start(bf16[1,2048,352]{1,2,0:T(8,128)(2,1)} %param.21) | copy-start | bytes 4325380
  401.7 1.8 copy-start.12
  595.1 106.4 %all-to-all-start.1 = ((bf16[32,32,2048]{2,1,0:T(8,128)(2,1)}), bf16[32,32,2048]{2,1,0:T(8,128)(2,1)}, u32[]{:S(2)}, u32[]{:S(2)}) async-start(bf16[32,32,2048]{2,1,0:T(8,128)(2,1)} %all-reduce.6.cloned.1.call-done), calls=%async_computation.1 | async-start | bytes 8388608 | tf_op jit(solution)/shard_map/all_to_all | solution.py:127
  707.0 4.6 copy-start.10
Sparse Core Ops, SparseCore 0:
  9.1 46.1 all-gather.3
  60.4 112.2 all-gather.5
  209.4 77.4 all-reduce.3
  410.1 184.8 all-reduce.5
